TPU v7x, 32 devices: a whole 2x2x4 slice. The times are simulated.
32 devices in a mesh: dom: 8 (over z, y), group: 4 (over x, core).
Axes of the slice: x: 2, y: 2, z: 4, core: 2. Of those that a mesh axis runs over, the one named last changes fastest.
Arguments:
- features: bfloat16 [4096, 1024], P(('dom', 'group')), may hold values from -6 to 6
- out_grad: bfloat16 [4096, 1024], P(('dom', 'group')), may hold values from -0.1796875 to 0.1796875
- gcn_weight: bfloat16 [1024, 1024], replicated, may hold values from -0.1875 to 0.1875
- tile_index: int32 [32, 4], P(('dom', 'group')), may hold values from 0 to 2
- tile_edges: int32 [32, 4, 128, 128], P(('dom', 'group')), may hold values 0 or 1
- halo_rows: int32 [8, 4, 8, 32], P('dom', 'group'), may hold values from 0 to 127
- routes: int32 [4096, 2], P(('dom', 'group')), may hold values from 0 to 15, all different within a row; in each aligned block of 128 rows (0 to 127, 128 to 255, ...) at most 20 rows name the same one
- route_weight: float32 [4096, 2], P(('dom', 'group')), may hold values from 0.25 to 1
- up_weight: bfloat16 [16, 1024, 4096], P('dom', None, 'group'), may hold values from -0.1875 to 0.1875
- down_weight: bfloat16 [16, 4096, 1024], P('dom', 'group'), may hold values from -0.09375 to 0.09375
Outputs:
- node_out: bfloat16 [4096, 1024], P(('dom', 'group'))
- up_grad: bfloat16 [16, 1024, 4096], P('dom', None, 'group')
- down_grad: bfloat16 [16, 4096, 1024], P('dom', 'group')
Inputs may be any that keep to these rules, and one draw needn't show every extreme that they name: `routes`: in the rows of one partition no expert is named more than 20 times, and in every draw some partition names some expert exactly 20 times.
All inputs are finite; a program needn't handle non-finite values. No bound on the sum of `tile_edges` on one device may be relied on, other than what follows from the above.
Results may differ from a plain program's by a relative error of at most 0.0071.
Values may be sent and summed in bfloat16 or wider, within the bound.
A program may use at most 128 MiB of HBM per device.

v0:
```python
import jax
import jax.numpy as jnp
from jax import lax
from jax.sharding import PartitionSpec as P


def silu_slope(values):
    logistic = jax.nn.sigmoid(values)
    return logistic * (1.0 + values * (1.0 - logistic))


def slot_table(route_rows, expert_count, capacity):
    flat_ids = route_rows.reshape(-1)
    onehot = (flat_ids[:, None] == jnp.arange(expert_count, dtype=jnp.int32)[None, :]).astype(
        jnp.int32
    )
    before = jnp.cumsum(onehot, axis=0) - onehot
    within = jnp.sum(before * onehot, axis=1)
    target = flat_ids * capacity + within
    filler = (
        jnp.zeros((expert_count * capacity,), jnp.int32)
        .at[target]
        .set(jnp.arange(flat_ids.shape[0], dtype=jnp.int32) + 1)
    )
    return (target, filler)


def local(
    features,
    out_grad,
    gcn_weight,
    tile_index,
    tile_edges,
    halo_rows,
    routes,
    route_weight,
    up_weight,
    down_weight,
):
    dom_count = lax.axis_size("dom")
    group_count = lax.axis_size("group")
    node_count, width = features.shape
    tile_rows = tile_edges.shape[-1]
    local_tiles = tile_index.shape[0]
    border_rows = halo_rows.shape[-1]
    expert_local = up_weight.shape[0]
    expert_count = expert_local * dom_count
    top_count = routes.shape[1]
    capacity = max(2, 5 * node_count * top_count // (4 * expert_count))
    send_lists = halo_rows.reshape(-1)
    outgoing = features[send_lists].reshape(dom_count, border_rows, width)
    incoming = lax.all_to_all(outgoing, "dom", split_axis=0, concat_axis=0, tiled=True)
    sources = jnp.concatenate(
        [features, incoming.reshape(dom_count * border_rows, width)], axis=0
    ).reshape(-1, tile_rows, width)
    chosen = sources[tile_index]
    edge_values = tile_edges.astype(jnp.bfloat16)
    summed = features.reshape(local_tiles, tile_rows, width).astype(jnp.float32) + jnp.einsum(
        "tsij,tsjd->tid", edge_values, chosen, preferred_element_type=jnp.float32
    )
    degree = 1.0 + jnp.sum(tile_edges, axis=(1, 3)).astype(jnp.float32)
    aggregated = (
        (summed / jnp.sqrt(degree)[:, :, None]).reshape(node_count, width).astype(jnp.bfloat16)
    )
    preact = jnp.dot(aggregated, gcn_weight, preferred_element_type=jnp.float32)
    hidden = (features.astype(jnp.float32) + jax.nn.silu(preact)).astype(jnp.bfloat16)
    targets, fillers = slot_table(routes, expert_count, capacity)
    cotangent = (
        (route_weight[:, :, None] * out_grad[:, None, :].astype(jnp.float32))
        .astype(jnp.bfloat16)
        .reshape(-1, width)
    )
    present = (fillers > 0)[:, None]
    source_pair = jnp.maximum(fillers - 1, 0)
    nothing = jnp.zeros((), jnp.bfloat16)
    slot_shape = (dom_count, expert_local * capacity, width)
    send_hidden = jnp.where(present, hidden[source_pair // top_count], nothing).reshape(slot_shape)
    send_cot = jnp.where(present, cotangent[source_pair], nothing).reshape(slot_shape)
    stack_hidden, stack_cot = (
        lax.all_gather(send_hidden[None], "group", axis=0, tiled=True),
        lax.all_gather(send_cot[None], "group", axis=0, tiled=True),
    )
    token_hidden, token_cot = (
        lax.all_to_all(stack_hidden, "dom", split_axis=1, concat_axis=1, tiled=True),
        lax.all_to_all(stack_cot, "dom", split_axis=1, concat_axis=1, tiled=True),
    )
    sender_count = group_count * dom_count
    token_hidden = token_hidden.reshape(sender_count, expert_local, capacity, width)
    token_cot = token_cot.reshape(sender_count, expert_local, capacity, width)
    up_proj = jnp.einsum(
        "secd,edf->secf", token_hidden, up_weight, preferred_element_type=jnp.float32
    )
    active = jax.nn.silu(up_proj).astype(jnp.bfloat16)
    merged = lax.psum_scatter(
        jnp.einsum(
            "secf,efd->secd", active, down_weight, preferred_element_type=jnp.float32
        ).astype(jnp.bfloat16),
        "group",
        scatter_dimension=0,
        tiled=True,
    )
    expert_out = merged.reshape(dom_count, expert_local * capacity, width)
    returned = lax.all_to_all(expert_out, "dom", split_axis=0, concat_axis=0, tiled=True).reshape(
        expert_count * capacity, width
    )
    gathered = returned[targets].reshape(node_count, top_count, width)
    node_out = (
        hidden.astype(jnp.float32)
        + jnp.sum(route_weight[:, :, None] * gathered.astype(jnp.float32), axis=1)
    ).astype(jnp.bfloat16)
    grad_act = jnp.einsum(
        "secd,efd->secf", token_cot, down_weight, preferred_element_type=jnp.float32
    )
    grad_pre = (grad_act * silu_slope(up_proj)).astype(jnp.bfloat16)
    down_grad = jnp.einsum(
        "secf,secd->efd", active, token_cot, preferred_element_type=jnp.float32
    ).astype(jnp.bfloat16)
    up_grad = jnp.einsum(
        "secd,secf->edf", token_hidden, grad_pre, preferred_element_type=jnp.float32
    ).astype(jnp.bfloat16)
    return (node_out, up_grad, down_grad)


def solution(mesh):
    in_specs = (
        P(("dom", "group"), None),
        P(("dom", "group"), None),
        P(),
        P(("dom", "group"), None),
        P(("dom", "group"), None, None, None),
        P("dom", "group", None, None),
        P(("dom", "group"), None),
        P(("dom", "group"), None),
        P("dom", None, "group"),
        P("dom", "group", None),
    )
    out_specs = (P(("dom", "group"), None), P("dom", None, "group"), P("dom", "group", None))
    return jax.shard_map(local, mesh=mesh, in_specs=in_specs, out_specs=out_specs, check_vma=False)
```

profile of v0, /device:TPU:13, one launch (start us, length us, event | category | flops | bytes accessed | tf_op | source)
XLA Modules:
  0.0 252.4 jit_solution(12656710248381427946)
XLA Ops:
  8.2 3.3 %gather_fusion = bf16[256,1024]{1,0:T(8,128)(2,1)} fusion(bf16[128,1024]{1,0:T(8,128)(2,1)} %param.10, s32[1024]{0:T(1024)S(1)} %pad_clamp_fusion.4), kind=kCustom, calls=%fused_computation | custom fusion | bytes 1049600 | tf_op jit(solution)/shard_map/gather | solution.py:51
  11.5 5.7 %all-to-all-start = ((bf16[8,32,1024]{2,1,0:T(8,128)(2,1)}), bf16[8,32,1024]{2,1,0:T(8,128)(2,1)}, u32[]{:S(2)}, u32[]{:S(2)}) async-start(bf16[8,32,1024]{2,1,0:T(8,128)(2,1)} %bitcast.1), calls=%async_computation | async-start | bytes 1048576 | tf_op jit(solution)/shard_map/all_to_all | solution.py:52
  18.8 1.4 scatter_custom_fusion
  22.3 1.7 mul.73
  25.4 1.3 multiply_convert_fusion
  26.8 2.6 %gather_fusion.4 = bf16[320,1024]{1,0:T(8,128)(2,1)} fusion(bf16[256,1024]{1,0:T(8,128)(2,1)S(1)} %multiply_convert_fusion, s32[1024]{0:T(1024)S(1)} %get-tuple-element.16), kind=kCustom, calls=%fused_computation.4 | custom fusion | bytes 1312000 | tf_op jit(solution)/shard_map/gather | solution.py:78
  30.5 1.6 gather_fusion.1
  32.1 3.0 %fusion.24 = bf16[128,1024]{0,1:T(8,128)(2,1)S(1)} fusion(bf16[128,1024]{0,1:T(8,128)(2,1)} %copy.60, bf16[1024,1024]{1,0:T(8,128)(2,1)S(1)} %copy-done, bf16[4,128,1024]{2,1,0:T(8,128)(2,1)} %gather_fusion.1, f32[128]{0:T(128)S(1)} %add_sqrt_fusion, s32[1,4,128,128]{3,2,1,0:T(8,128)} %param.14), kind=kOutput, calls=%fused_computation.38 | convolution fusion | flops 404160512 | bytes 3932672 | tf_op jit(solution)/shard_map/dot_general | solution.py:65
  35.2 2.1 gather_fusion.2
  38.6 27.6 %all-gather.3.cloned.1.call-done = bf16[4,8,40,1024]{3,2,1,0:T(8,128)(2,1)} async-done(((bf16[1,8,40,1024]{3,2,1,0:T(8,128)(2,1)}), bf16[4,8,40,1024]{3,2,1,0:T(8,128)(2,1)}) %all-gather.3.cloned.1.call-update) | async-done | bytes 2621456 | tf_op jit(solution)/shard_map/all_gather | solution.py:80
  66.2 5.3 %copy.70 = bf16[4,8,40,1024]{3,0,2,1:T(4,128)(2,1)} copy(bf16[4,8,40,1024]{3,2,1,0:T(8,128)(2,1)} %all-gather.3.cloned.1.call-done) | data formatting | bytes 5242880 | tf_op jit(solution)/shard_map/all_gather | solution.py:80
  71.4 5.5 %all-to-all-start.1 = ((bf16[4,8,40,1024]{3,0,2,1:T(4,128)(2,1)}), bf16[4,8,40,1024]{3,0,2,1:T(4,128)(2,1)S(1)}, u32[]{:S(2)}, u32[]{:S(2)}) async-start(bf16[4,8,40,1024]{3,0,2,1:T(4,128)(2,1)} %copy.70), calls=%async_computation.1 | async-start | bytes 5242880 | tf_op jit(solution)/shard_map/all_to_all | solution.py:84
  77.6 28.3 %all-gather.5.cloned.1.call-done = bf16[4,8,40,1024]{3,2,1,0:T(8,128)(2,1)} async-done(((bf16[1,8,40,1024]{3,2,1,0:T(8,128)(2,1)}), bf16[4,8,40,1024]{3,2,1,0:T(8,128)(2,1)}) %all-gather.5.cloned.1.call-update) | async-done | bytes 2621456 | tf_op jit(solution)/shard_map/all_gather | solution.py:81
  106.0 5.3 %copy.75 = bf16[4,8,40,1024]{3,0,2,1:T(4,128)(2,1)} copy(bf16[4,8,40,1024]{3,2,1,0:T(8,128)(2,1)} %all-gather.5.cloned.1.call-done) | data formatting | bytes 5242880 | tf_op jit(solution)/shard_map/all_gather | solution.py:81
  111.3 22.6 %all-to-all-done.1 = bf16[4,8,40,1024]{3,0,2,1:T(4,128)(2,1)S(1)} async-done(((bf16[4,8,40,1024]{3,0,2,1:T(4,128)(2,1)}), bf16[4,8,40,1024]{3,0,2,1:T(4,128)(2,1)S(1)}, u32[]{:S(2)}, u32[]{:S(2)}) %all-to-all-start.1) | async-done | bytes 2621472 | tf_op jit(solution)/shard_map/all_to_all | solution.py:84
  133.8 6.4 %all-to-all-start.3 = ((bf16[4,8,40,1024]{3,0,2,1:T(4,128)(2,1)}), bf16[4,8,40,1024]{3,0,2,1:T(4,128)(2,1)}, u32[]{:S(2)}, u32[]{:S(2)}) async-start(bf16[4,8,40,1024]{3,0,2,1:T(4,128)(2,1)} %copy.75), calls=%async_computation.3 | async-start | bytes 5242880 | tf_op jit(solution)/shard_map/all_to_all | solution.py:85
  140.3 2.8 %copy.71 = bf16[4,8,40,1024]{3,1,0,2:T(8,128)(2,1)S(1)} copy(bf16[4,8,40,1024]{3,0,2,1:T(4,128)(2,1)S(1)} %all-to-all-done.1) | data formatting | bytes 5242880 | tf_op jit(solution)/shard_map/all_to_all | solution.py:84
  143.1 1.5 copy-done.3
  144.6 2.9 %fusion.7 = f32[2,32,20,1024]{3,1,2,0:T(8,128)S(1)} fusion(bf16[32,2,20,1024]{3,0,2,1:T(8,128)(2,1)S(1)} %bitcast.122, bf16[2,1024,1024]{2,1,0:T(8,128)(2,1)S(1)} %copy-done.8), kind=kOutput, calls=%fused_computation.19 | convolution fusion | flops 2684354560 | bytes 12058624 | tf_op jit(solution)/shard_map/secd,edf->secf/dot_general | solution.py:90
  147.5 3.4 %convert_bitcast_fusion = bf16[32,2,20,1024]{3,0,2,1:T(8,128)(2,1)S(1)} fusion(bf16[2,1024,1024]{2,1,0:T(8,128)(2,1)S(1)} %copy-done.9, f32[2,32,20,1024]{3,1,2,0:T(8,128)S(1)} %fusion.7), kind=kOutput, calls=%fused_computation.25 | convolution fusion | flops 2692218880 | bytes 12058624 | tf_op jit(solution)/shard_map/secf,efd->secd/dot_general | solution.py:95
  150.8 1.5 copy.84
  152.3 3.0 %reshape.242 = bf16[32,40960]{1,0:T(8,128)(2,1)} reshape(bf16[32,2,20,1024]{3,2,1,0:T(8,128)(2,1)S(1)} %copy.84) | data formatting | bytes 5242880
  155.3 41.8 %all-to-all-done.3 = bf16[4,8,40,1024]{3,0,2,1:T(4,128)(2,1)} async-done(((bf16[4,8,40,1024]{3,0,2,1:T(4,128)(2,1)}), bf16[4,8,40,1024]{3,0,2,1:T(4,128)(2,1)}, u32[]{:S(2)}, u32[]{:S(2)}) %all-to-all-start.3) | async-done | bytes 2621472 | tf_op jit(solution)/shard_map/all_to_all | solution.py:85
  197.2 6.1 %copy.76 = bf16[4,8,40,1024]{3,1,0,2:T(8,128)(2,1)} copy(bf16[4,8,40,1024]{3,0,2,1:T(4,128)(2,1)} %all-to-all-done.3) | data formatting | bytes 5242880 | tf_op jit(solution)/shard_map/all_to_all | solution.py:85
  203.3 11.0 %bitcast_convert_fusion.1 = bf16[2,1024,1024]{2,1,0:T(8,128)(2,1)} fusion(bf16[32,2,20,1024]{3,0,2,1:T(8,128)(2,1)S(1)} %bitcast.123, f32[2,32,20,1024]{3,1,2,0:T(8,128)} %copy-done.11, bf16[32,2,20,1024]{3,0,2,1:T(8,128)(2,1)} %bitcast.124, bf16[2,1024,1024]{2,1,0:T(8,128)(2,1)} %param.19), kind=kOutput, calls=%fused_computation.7 | convolution fusion | flops 5382602752 | bytes 18874368 | tf_op jit(solution)/shard_map/secd,secf->edf/dot_general | solution.py:118
  214.3 2.3 copy.72
  216.7 6.5 %all-to-all-start.2 = ((bf16[8,40,1024]{2,1,0:T(8,128)(2,1)}), bf16[8,40,1024]{2,1,0:T(8,128)(2,1)S(1)}, u32[]{:S(2)}, u32[]{:S(2)}) async-start(bf16[8,40,1024]{2,1,0:T(8,128)(2,1)} %copy.72), calls=%async_computation.2 | async-start | bytes 1310720 | tf_op jit(solution)/shard_map/all_to_all | solution.py:103
  223.1 8.9 %bitcast_convert_fusion = bf16[2,1024,1024]{2,1,0:T(8,128)(2,1)} fusion(bf16[32,2,20,1024]{3,0,2,1:T(8,128)(2,1)} %bitcast.125, f32[2,32,20,1024]{3,1,2,0:T(8,128)} %copy-done.11), kind=kOutput, calls=%fused_computation.6 | convolution fusion | flops 2693005312 | bytes 12058624 | tf_op jit(solution)/shard_map/secf,secd->efd/dot_general | solution.py:115
  232.0 5.9 %all-to-all-done.2 = bf16[8,40,1024]{2,1,0:T(8,128)(2,1)S(1)} async-done(((bf16[8,40,1024]{2,1,0:T(8,128)(2,1)}), bf16[8,40,1024]{2,1,0:T(8,128)(2,1)S(1)}, u32[]{:S(2)}, u32[]{:S(2)}) %all-to-all-start.2) | async-done | bytes 655392 | tf_op jit(solution)/shard_map/all_to_all | solution.py:103
  237.9 2.0 gather_fusion.3
  239.8 1.7 reshape.184
  241.5 2.1 multiply_reduce_fusion
  (67 shorter events, 11.4 us)
Async XLA Ops:
  7.2 25.0 %copy-start = (bf16[1024,1024]{1,0:T(8,128)(2,1)S(1)}, bf16[1024,1024]{1,0:T(8,128)(2,1)}, u32[]{:S(2)}) copy-start(bf16[1024,1024]{1,0:T(8,128)(2,1)} %param.12) | copy-start | bytes 6291460
  7.2 13.0 %copy-start.2 = (bf16[128,1024]{1,0:T(8,128)(2,1)S(1)}, bf16[128,1024]{1,0:T(8,128)(2,1)}, u32[]{:S(2)}) copy-start(bf16[128,1024]{1,0:T(8,128)(2,1)} %param.10) | copy-start | bytes 786436
  7.2 10.0 %copy-start.6 = (s32[128,2]{0,1:T(2,128)S(1)}, s32[128,2]{0,1:T(2,128)}, u32[]{:S(2)}) copy-start(s32[128,2]{0,1:T(2,128)} %param.16) | copy-start | bytes 3076
  8.1 15.8 %copy-start.7 = (f32[128,2]{0,1:T(2,128)S(1)}, f32[128,2]{0,1:T(2,128)}, u32[]{:S(2)}) copy-start(f32[128,2]{0,1:T(2,128)} %param.17) | copy-start | bytes 3076
  11.5 17.9 %all-to-all-start = ((bf16[8,32,1024]{2,1,0:T(8,128)(2,1)}), bf16[8,32,1024]{2,1,0:T(8,128)(2,1)}, u32[]{:S(2)}, u32[]{:S(2)}) async-start(bf16[8,32,1024]{2,1,0:T(8,128)(2,1)} %bitcast.1), calls=%async_computation | async-start | bytes 1048576 | tf_op jit(solution)/shard_map/all_to_all | solution.py:52
  17.1 49.0 %all-gather.3.cloned.1.call-start = ((), (), s32[]{:S(2)}) async-start(), calls=%async_computation.5 | async-start | bytes 3276800 | tf_op jit(solution)/shard_map/all_gather | solution.py:80
  24.0 5.4 %copy-start.10 = (s32[1,4]{1,0:T(1,128)S(1)}, s32[1,4]{1,0:T(1,128)}, u32[]{:S(2)}) copy-start(s32[1,4]{1,0:T(1,128)} %param.13) | copy-start | bytes 52
  35.1 2.3 copy-start.5
  71.4 62.4 %all-to-all-start.1 = ((bf16[4,8,40,1024]{3,0,2,1:T(4,128)(2,1)}), bf16[4,8,40,1024]{3,0,2,1:T(4,128)(2,1)S(1)}, u32[]{:S(2)}, u32[]{:S(2)}) async-start(bf16[4,8,40,1024]{3,0,2,1:T(4,128)(2,1)} %copy.70), calls=%async_computation.1 | async-start | bytes 5242880 | tf_op jit(solution)/shard_map/all_to_all | solution.py:84
  76.9 29.1 %all-gather.5.cloned.1.call-start = ((), (), s32[]{:S(2)}) async-start(), calls=%async_computation.6 | async-start | bytes 3276800 | tf_op jit(solution)/shard_map/all_gather | solution.py:81
  133.8 63.4 %all-to-all-start.3 = ((bf16[4,8,40,1024]{3,0,2,1:T(4,128)(2,1)}), bf16[4,8,40,1024]{3,0,2,1:T(4,128)(2,1)}, u32[]{:S(2)}, u32[]{:S(2)}) async-start(bf16[4,8,40,1024]{3,0,2,1:T(4,128)(2,1)} %copy.75), calls=%async_computation.3 | async-start | bytes 5242880 | tf_op jit(solution)/shard_map/all_to_all | solution.py:85
  140.3 74.1 %reduce-scatter.4.cloned.1.call-start = ((), (), s32[]{:S(2)}) async-start(), calls=%async_computation.7 | async-start | bytes 3276800
  140.3 4.3 %copy-start.8 = (bf16[2,1024,1024]{2,1,0:T(8,128)(2,1)S(1)}, bf16[2,1024,1024]{2,1,0:T(8,128)(2,1)}, u32[]{:S(2)}) copy-start(bf16[2,1024,1024]{2,1,0:T(8,128)(2,1)} %param.18) | copy-start | bytes 12582916
  143.1 1.5 copy-start.3
  144.6 2.9 %copy-start.9 = (bf16[2,1024,1024]{2,1,0:T(8,128)(2,1)S(1)}, bf16[2,1024,1024]{2,1,0:T(8,128)(2,1)}, u32[]{:S(2)}) copy-start(bf16[2,1024,1024]{2,1,0:T(8,128)(2,1)} %param.19) | copy-start | bytes 12582916
  147.4 3.4 %copy-start.11 = (f32[2,32,20,1024]{3,1,2,0:T(8,128)}, f32[2,32,20,1024]{3,1,2,0:T(8,128)S(1)}, u32[]{:S(2)}) copy-start(f32[2,32,20,1024]{3,1,2,0:T(8,128)S(1)} %fusion.7) | copy-start | bytes 15728644
  155.3 48.0 %copy-start.4 = (bf16[4,8,40,1024]{3,1,0,2:T(8,128)(2,1)S(1)}, bf16[4,8,40,1024]{3,1,0,2:T(8,128)(2,1)}, u32[]{:S(2)}) copy-start(bf16[4,8,40,1024]{3,1,0,2:T(8,128)(2,1)} %copy-done.3) | copy-start | bytes 7864324
  216.7 21.2 %all-to-all-start.2 = ((bf16[8,40,1024]{2,1,0:T(8,128)(2,1)}), bf16[8,40,1024]{2,1,0:T(8,128)(2,1)S(1)}, u32[]{:S(2)}, u32[]{:S(2)}) async-start(bf16[8,40,1024]{2,1,0:T(8,128)(2,1)} %copy.72), calls=%async_computation.2 | async-start | bytes 1310720 | tf_op jit(solution)/shard_map/all_to_all | solution.py:103
  237.9 8.0 %copy-start.1 = (bf16[1024,1024]{1,0:T(8,128)(2,1)S(1)}, bf16[1024,1024]{1,0:T(8,128)(2,1)}, u32[]{:S(2)}) copy-start(bf16[1024,1024]{1,0:T(8,128)(2,1)} %param.12) | copy-start | bytes 6291460
Sparse Core Ops, SparseCore 0:
  38.7 27.3 all-gather.2
  79.9 26.0 all-gather.4
  155.5 35.6 reduce-scatter.3
where the time goes:
time: 257 us; the launch traced here: 252 us
  waiting for transfers between devices  127 us (49%)
  local copies, waits for them, and re-layouts  50.6 us (20%)
  matrix products  29.1 us (11%)
  starting transfers between devices  24 us (9%)
  between operations  14 us (5%)
  other arithmetic  7.72 us (3%)
    all_to_all x1, waiting for transfers between devices, local(): lax.all_to_all(stack_cot, 'dom', split_axis=1, concat_axis=1, tiled=True)  41.8 us
    all_gather x1, waiting for transfers between devices, local(): lax.all_gather(send_cot[None], 'group', axis=0, tiled=True)  28.3 us
    all_gather x1, waiting for transfers between devices, local(): lax.all_gather(send_hidden[None], 'group', axis=0, tiled=True)  27.6 us
    all_to_all x1, waiting for transfers between devices, local(): lax.all_to_all(stack_hidden, 'dom', split_axis=1, concat_axis=1, tiled=True)  22.6 us
    dot_general x1, matrix products, local(): jnp.einsum('secd,secf->edf', token_hidden, grad_pre, preferred_element_ty...  11 us
    dot_general x1, matrix products, local(): jnp.einsum('secf,secd->efd', active, token_cot, preferred_element_type=jn...  8.86 us
    unnamed x30, local copies, waits for them, and re-layouts  7.92 us
    all_to_all x1, starting transfers between devices, local(): lax.all_to_all(expert_out, 'dom', split_axis=0, concat_axis=0, tiled=True)  6.46 us
  transfers between devices with their start and end apart: 7, of which 5 were waited for; matrix products, arithmetic and copies ran while one was open for 23% of the time, Pallas kernels for 0%

commit v1 on v0

--- a/solution.py
+++ b/solution.py
@@ -76,14 +76,10 @@
     slot_shape = (dom_count, expert_local * capacity, width)
     send_hidden = jnp.where(present, hidden[source_pair // top_count], nothing).reshape(slot_shape)
     send_cot = jnp.where(present, cotangent[source_pair], nothing).reshape(slot_shape)
-    stack_hidden, stack_cot = (
-        lax.all_gather(send_hidden[None], "group", axis=0, tiled=True),
-        lax.all_gather(send_cot[None], "group", axis=0, tiled=True),
-    )
-    token_hidden, token_cot = (
-        lax.all_to_all(stack_hidden, "dom", split_axis=1, concat_axis=1, tiled=True),
-        lax.all_to_all(stack_cot, "dom", split_axis=1, concat_axis=1, tiled=True),
-    )
+    mine_cot = lax.all_to_all(send_cot, "dom", split_axis=0, concat_axis=0, tiled=True)
+    token_cot = lax.all_gather(mine_cot[None], "group", axis=0, tiled=True)
+    mine_hidden = lax.all_to_all(send_hidden, "dom", split_axis=0, concat_axis=0, tiled=True)
+    token_hidden = lax.all_gather(mine_hidden[None], "group", axis=0, tiled=True)
     sender_count = group_count * dom_count
     token_hidden = token_hidden.reshape(sender_count, expert_local, capacity, width)
     token_cot = token_cot.reshape(sender_count, expert_local, capacity, width)

time: 257 us -> 194 us (0.75)
  the two profiles are of different devices: /device:TPU:13 before, /device:TPU:0 now
where the time goes in v1:
time: 194 us; the launch traced here: 193 us
  local copies, waits for them, and re-layouts  43.4 us (22%)
  waiting for transfers between devices  42.6 us (22%)
  blocking collectives  42.1 us (22%)
  matrix products  30 us (15%)
  between operations  14 us (7%)
  starting transfers between devices  13.1 us (7%)
  other arithmetic  7.74 us (4%)
    all_to_all x1, blocking collectives, local(): lax.all_to_all(send_hidden, 'dom', split_axis=0, concat_axis=0, tiled=True)  21.4 us
    all_to_all x1, blocking collectives, local(): lax.all_to_all(send_cot, 'dom', split_axis=0, concat_axis=0, tiled=True)  20.7 us
    unnamed x4, waiting for transfers between devices  20.4 us
    dot_general x1, matrix products, local(): jnp.einsum('secd,secf->edf', token_hidden, grad_pre, preferred_element_ty...  12.2 us
    unnamed x32, local copies, waits for them, and re-layouts  11.6 us
    dot_general x1, matrix products, local(): jnp.einsum('secf,secd->efd', active, token_cot, preferred_element_type=jn...  8.86 us
    all_to_all x1, waiting for transfers between devices, local(): lax.all_to_all(expert_out, 'dom', split_axis=0, concat_axis=0, tiled=True)  8.44 us
    all_gather x1, waiting for transfers between devices, local(): token_cot = lax.all_gather(mine_cot[None], 'group', axis=0, tiled=True)  8.1 us
  transfers between devices with their start and end apart: 5, of which 5 were waited for; matrix products, arithmetic and copies ran while one was open for 29% of the time, Pallas kernels for 0%

profile of v1, /device:TPU:0, one launch (start us, length us, event | category | flops | bytes accessed | tf_op | source)
XLA Modules:
  0.0 192.9 jit_solution(4663778561806008242)
XLA Ops:
  8.2 3.3 %gather_fusion = bf16[256,1024]{1,0:T(8,128)(2,1)} fusion(bf16[128,1024]{1,0:T(8,128)(2,1)} %param.10, s32[1024]{0:T(1024)S(1)} %pad_clamp_fusion.4), kind=kCustom, calls=%fused_computation | custom fusion | bytes 1049600 | tf_op jit(solution)/shard_map/gather | solution.py:51
  11.5 7.3 %all-to-all-start = ((bf16[8,32,1024]{2,1,0:T(8,128)(2,1)}), bf16[8,32,1024]{2,1,0:T(8,128)(2,1)}, u32[]{:S(2)}, u32[]{:S(2)}) async-start(bf16[8,32,1024]{2,1,0:T(8,128)(2,1)} %bitcast.1), calls=%async_computation | async-start | bytes 1048576 | tf_op jit(solution)/shard_map/all_to_all | solution.py:52
  20.4 1.4 scatter_custom_fusion
  24.0 1.7 mul.73
  27.1 1.3 multiply_convert_fusion
  28.4 2.6 %gather_fusion.4 = bf16[320,1024]{1,0:T(8,128)(2,1)} fusion(bf16[256,1024]{1,0:T(8,128)(2,1)S(1)} %multiply_convert_fusion, s32[1024]{0:T(1024)S(1)} %get-tuple-element.16), kind=kCustom, calls=%fused_computation.4 | custom fusion | bytes 1312000 | tf_op jit(solution)/shard_map/gather | solution.py:78
  31.1 2.3 %all-to-all-done = bf16[8,32,1024]{2,1,0:T(8,128)(2,1)} async-done(((bf16[8,32,1024]{2,1,0:T(8,128)(2,1)}), bf16[8,32,1024]{2,1,0:T(8,128)(2,1)}, u32[]{:S(2)}, u32[]{:S(2)}) %all-to-all-start) | async-done | bytes 524320 | tf_op jit(solution)/shard_map/all_to_all | solution.py:52
  34.5 1.6 gather_fusion.1
  36.1 2.9 %fusion.24 = bf16[128,1024]{0,1:T(8,128)(2,1)S(1)} fusion(bf16[128,1024]{0,1:T(8,128)(2,1)} %copy.56, bf16[1024,1024]{1,0:T(8,128)(2,1)S(1)} %copy-done, bf16[4,128,1024]{2,1,0:T(8,128)(2,1)} %gather_fusion.1, f32[128]{0:T(128)S(1)} %add_sqrt_fusion, s32[1,4,128,128]{3,2,1,0:T(8,128)S(1)} %copy-done.6), kind=kOutput, calls=%fused_computation.38 | convolution fusion | flops 404160512 | bytes 3932672 | tf_op jit(solution)/shard_map/dot_general | solution.py:65
  39.1 2.6 %gather_fusion.2 = bf16[320,1024]{1,0:T(8,128)(2,1)} fusion(bf16[128,1024]{1,0:T(8,128)(2,1)S(1)} %copy.65, s32[1024]{0:T(1024)S(1)} %get-tuple-element.17), kind=kCustom, calls=%fused_computation.2 | custom fusion | bytes 1312000 | tf_op jit(solution)/shard_map/gather | solution.py:77
  41.8 1.2 broadcast_select_fusion
  43.0 21.4 %all_to_all.20 = bf16[8,40,1024]{2,1,0:T(8,128)(2,1)} all-to-all(bf16[8,40,1024]{2,1,0:T(8,128)(2,1)S(1)} %get-tuple-element.15), channel_id=1, replica_groups=mesh['dom'=8,'group'=4] {'dom'}, dimensions={0} | all-to-all | bytes 1310720 | tf_op jit(solution)/shard_map/all_to_all | solution.py:81
  64.5 20.7 %all_to_all.21 = bf16[8,40,1024]{2,1,0:T(8,128)(2,1)} all-to-all(bf16[8,40,1024]{2,1,0:T(8,128)(2,1)S(1)} %get-tuple-element.14), channel_id=1, replica_groups=mesh['dom'=8,'group'=4] {'dom'}, dimensions={0} | all-to-all | bytes 1310720 | tf_op jit(solution)/shard_map/all_to_all | solution.py:79
  85.4 3.4 %all-gather.5.cloned.1.call-done = bf16[32,40,1024]{2,1,0:T(8,128)(2,1)} async-done(((bf16[8,40,1024]{2,1,0:T(8,128)(2,1)}), bf16[32,40,1024]{2,1,0:T(8,128)(2,1)}) %all-gather.5.cloned.1.call-update) | async-done | bytes 2621456 | tf_op jit(solution)/shard_map/all_gather | solution.py:82
  88.8 3.3 %copy.66 = bf16[32,40,1024]{2,0,1:T(8,128)(2,1)S(1)} copy(bf16[32,40,1024]{2,1,0:T(8,128)(2,1)} %all-gather.5.cloned.1.call-done) | data formatting | bytes 5242880 | tf_op jit(solution)/shard_map/all_gather | solution.py:82
  92.2 1.5 copy-done.2
  93.7 2.9 %fusion.7 = f32[2,32,20,1024]{3,1,2,0:T(8,128)S(1)} fusion(bf16[32,2,20,1024]{3,0,2,1:T(8,128)(2,1)S(1)} %bitcast.122, bf16[2,1024,1024]{2,1,0:T(8,128)(2,1)S(1)} %copy-done.9), kind=kOutput, calls=%fused_computation.19 | convolution fusion | flops 2684354560 | bytes 12058624 | tf_op jit(solution)/shard_map/secd,edf->secf/dot_general | solution.py:86
  96.6 3.1 %convert_bitcast_fusion = bf16[32,2,20,1024]{3,0,2,1:T(8,128)(2,1)S(1)} fusion(bf16[2,1024,1024]{2,1,0:T(8,128)(2,1)S(1)} %copy-done.10, f32[2,32,20,1024]{3,1,2,0:T(8,128)S(1)} %fusion.7), kind=kOutput, calls=%fused_computation.25 | convolution fusion | flops 2692218880 | bytes 12058624 | tf_op jit(solution)/shard_map/secf,efd->secd/dot_general | solution.py:91
  99.8 3.1 %copy.78 = bf16[32,2,20,1024]{3,2,1,0:T(8,128)(2,1)} copy(bf16[32,2,20,1024]{3,0,2,1:T(8,128)(2,1)S(1)} %convert_bitcast_fusion) | data formatting | bytes 5242880
  102.9 4.9 %reshape.226 = bf16[32,40960]{1,0:T(8,128)(2,1)} reshape(bf16[32,2,20,1024]{3,2,1,0:T(8,128)(2,1)} %copy.78) | data formatting | bytes 5242880
  107.9 8.1 %all-gather.7.cloned.1.call-done = bf16[32,40,1024]{2,1,0:T(8,128)(2,1)} async-done(((bf16[8,40,1024]{2,1,0:T(8,128)(2,1)}), bf16[32,40,1024]{2,1,0:T(8,128)(2,1)}) %all-gather.7.cloned.1.call-update) | async-done | bytes 2621456 | tf_op jit(solution)/shard_map/all_gather | solution.py:80
  116.0 4.7 %copy.70 = bf16[32,40,1024]{2,0,1:T(8,128)(2,1)} copy(bf16[32,40,1024]{2,1,0:T(8,128)(2,1)} %all-gather.7.cloned.1.call-done) | data formatting | bytes 5242880 | tf_op jit(solution)/shard_map/all_gather | solution.py:80
  120.7 12.2 %bitcast_convert_fusion.1 = bf16[2,1024,1024]{2,1,0:T(8,128)(2,1)} fusion(bf16[32,2,20,1024]{3,0,2,1:T(8,128)(2,1)} %bitcast.123, f32[2,32,20,1024]{3,1,2,0:T(8,128)} %copy-done.12, bf16[32,2,20,1024]{3,0,2,1:T(8,128)(2,1)} %bitcast.124, bf16[2,1024,1024]{2,1,0:T(8,128)(2,1)} %param.19), kind=kOutput, calls=%fused_computation.7 | convolution fusion | flops 5382602752 | bytes 18874368 | tf_op jit(solution)/shard_map/secd,secf->edf/dot_general | solution.py:114
  132.9 20.3 %reduce-scatter.4.cloned.1.call-done = bf16[8,40960]{1,0:T(8,128)(2,1)} async-done(((bf16[32,40960]{1,0:T(8,128)(2,1)}), bf16[8,40960]{1,0:T(8,128)(2,1)}) %reduce-scatter.4.cloned.1.call-update) | async-done | bytes 655376
  153.2 2.3 %copy.67 = bf16[8,40,1024]{2,1,0:T(8,128)(2,1)} copy(bf16[8,40,1024]{2,0,1:T(8,128)(2,1)} %bitcast.128) | data formatting | bytes 1310720 | tf_op jit(solution)/shard_map/reshape | solution.py:98
  155.6 5.5 %all-to-all-start.2 = ((bf16[8,40,1024]{2,1,0:T(8,128)(2,1)}), bf16[8,40,1024]{2,1,0:T(8,128)(2,1)S(1)}, u32[]{:S(2)}, u32[]{:S(2)}) async-start(bf16[8,40,1024]{2,1,0:T(8,128)(2,1)} %copy.67), calls=%async_computation.2 | async-start | bytes 1310720 | tf_op jit(solution)/shard_map/all_to_all | solution.py:99
  161.1 8.9 %bitcast_convert_fusion = bf16[2,1024,1024]{2,1,0:T(8,128)(2,1)} fusion(bf16[32,2,20,1024]{3,0,2,1:T(8,128)(2,1)} %bitcast.125, f32[2,32,20,1024]{3,1,2,0:T(8,128)} %copy-done.12), kind=kOutput, calls=%fused_computation.6 | convolution fusion | flops 2693005312 | bytes 12058624 | tf_op jit(solution)/shard_map/secf,secd->efd/dot_general | solution.py:111
  169.9 8.4 %all-to-all-done.2 = bf16[8,40,1024]{2,1,0:T(8,128)(2,1)S(1)} async-done(((bf16[8,40,1024]{2,1,0:T(8,128)(2,1)}), bf16[8,40,1024]{2,1,0:T(8,128)(2,1)S(1)}, u32[]{:S(2)}, u32[]{:S(2)}) %all-to-all-start.2) | async-done | bytes 655392 | tf_op jit(solution)/shard_map/all_to_all | solution.py:99
  178.4 2.0 %gather_fusion.3 = bf16[256,1024]{1,0:T(8,128)(2,1)} fusion(bf16[320,1024]{1,0:T(8,128)(2,1)S(1)} %bitcast.120, s32[1024]{0:T(1024)S(1)} %pad_clamp_fusion.1), kind=kCustom, calls=%fused_computation.3 | custom fusion | bytes 1049600 | tf_op jit(solution)/shard_map/gather | solution.py:102
  180.3 1.7 reshape.164
  182.0 2.1 %multiply_reduce_fusion = f32[128,1024]{1,0:T(8,128)} fusion(f32[128,2,1024]{2,1,0:T(2,128)S(1)} %reshape.164, f32[128,2]{1,0:T(8,128)S(1)} %copy.60), kind=kLoop, calls=%fused_computation.32 | loop fusion | flops 393216 | bytes 1573888 | tf_op jit(solution)/shard_map/reduce_sum | solution.py:105
  184.2 1.2 copy.68
  (65 shorter events, 8.6 us)
Async XLA Ops:
  7.2 28.9 %copy-start = (bf16[1024,1024]{1,0:T(8,128)(2,1)S(1)}, bf16[1024,1024]{1,0:T(8,128)(2,1)}, u32[]{:S(2)}) copy-start(bf16[1024,1024]{1,0:T(8,128)(2,1)} %param.12) | copy-start | bytes 6291460
  7.2 14.7 %copy-start.1 = (bf16[128,1024]{1,0:T(8,128)(2,1)S(1)}, bf16[128,1024]{1,0:T(8,128)(2,1)}, u32[]{:S(2)}) copy-start(bf16[128,1024]{1,0:T(8,128)(2,1)} %param.10) | copy-start | bytes 786436
  7.2 11.6 %copy-start.7 = (s32[128,2]{0,1:T(2,128)S(1)}, s32[128,2]{0,1:T(2,128)}, u32[]{:S(2)}) copy-start(s32[128,2]{0,1:T(2,128)} %param.16) | copy-start | bytes 3076
  8.1 17.5 %copy-start.8 = (f32[128,2]{0,1:T(2,128)S(1)}, f32[128,2]{0,1:T(2,128)}, u32[]{:S(2)}) copy-start(f32[128,2]{0,1:T(2,128)} %param.17) | copy-start | bytes 3076
  11.5 21.9 %all-to-all-start = ((bf16[8,32,1024]{2,1,0:T(8,128)(2,1)}), bf16[8,32,1024]{2,1,0:T(8,128)(2,1)}, u32[]{:S(2)}, u32[]{:S(2)}) async-start(bf16[8,32,1024]{2,1,0:T(8,128)(2,1)} %bitcast.1), calls=%async_computation | async-start | bytes 1048576 | tf_op jit(solution)/shard_map/all_to_all | solution.py:52
  18.8 70.0 %all-gather.5.cloned.1.call-start = ((), (), s32[]{:S(2)}) async-start(), calls=%async_computation.5 | async-start | bytes 3276800 | tf_op jit(solution)/shard_map/all_gather | solution.py:82
  25.6 5.4 %copy-start.11 = (s32[1,4]{1,0:T(1,128)S(1)}, s32[1,4]{1,0:T(1,128)}, u32[]{:S(2)}) copy-start(s32[1,4]{1,0:T(1,128)} %param.13) | copy-start | bytes 52
  28.4 7.6 %copy-start.6 = (s32[1,4,128,128]{3,2,1,0:T(8,128)S(1)}, s32[1,4,128,128]{3,2,1,0:T(8,128)}, u32[]{:S(2)}) copy-start(s32[1,4,128,128]{3,2,1,0:T(8,128)} %param.14) | copy-start | bytes 786436
  38.9 2.8 %copy-start.4 = (bf16[128,1024]{0,1:T(8,128)(2,1)}, bf16[128,1024]{0,1:T(8,128)(2,1)S(1)}, u32[]{:S(2)}) copy-start(bf16[128,1024]{0,1:T(8,128)(2,1)S(1)} %fusion.24) | copy-start | bytes 786436
  38.9 2.8 %copy-start.3 = (bf16[320,1024]{1,0:T(8,128)(2,1)S(1)}, bf16[320,1024]{1,0:T(8,128)(2,1)}, u32[]{:S(2)}) copy-start(bf16[320,1024]{1,0:T(8,128)(2,1)} %gather_fusion.4) | copy-start | bytes 1966084
  64.4 51.5 %all-gather.7.cloned.1.call-start = ((), (), s32[]{:S(2)}) async-start(), calls=%async_computation.6 | async-start | bytes 3276800 | tf_op jit(solution)/shard_map/all_gather | solution.py:80
  85.2 68.0 %reduce-scatter.4.cloned.1.call-start = ((), (), s32[]{:S(2)}) async-start(), calls=%async_computation.7 | async-start | bytes 3276800
  88.8 4.9 %copy-start.9 = (bf16[2,1024,1024]{2,1,0:T(8,128)(2,1)S(1)}, bf16[2,1024,1024]{2,1,0:T(8,128)(2,1)}, u32[]{:S(2)}) copy-start(bf16[2,1024,1024]{2,1,0:T(8,128)(2,1)} %param.18) | copy-start | bytes 12582916
  92.1 1.5 copy-start.2
  93.7 2.9 %copy-start.10 = (bf16[2,1024,1024]{2,1,0:T(8,128)(2,1)S(1)}, bf16[2,1024,1024]{2,1,0:T(8,128)(2,1)}, u32[]{:S(2)}) copy-start(bf16[2,1024,1024]{2,1,0:T(8,128)(2,1)} %param.19) | copy-start | bytes 12582916
  96.6 3.2 %copy-start.12 = (f32[2,32,20,1024]{3,1,2,0:T(8,128)}, f32[2,32,20,1024]{3,1,2,0:T(8,128)S(1)}, u32[]{:S(2)}) copy-start(f32[2,32,20,1024]{3,1,2,0:T(8,128)S(1)} %fusion.7) | copy-start | bytes 15728644
  155.6 22.8 %all-to-all-start.2 = ((bf16[8,40,1024]{2,1,0:T(8,128)(2,1)}), bf16[8,40,1024]{2,1,0:T(8,128)(2,1)S(1)}, u32[]{:S(2)}, u32[]{:S(2)}) async-start(bf16[8,40,1024]{2,1,0:T(8,128)(2,1)} %copy.67), calls=%async_computation.2 | async-start | bytes 1310720 | tf_op jit(solution)/shard_map/all_to_all | solution.py:99
  178.4 7.0 %copy-start.5 = (bf16[128,1024]{0,1:T(8,128)(2,1)S(1)}, bf16[128,1024]{0,1:T(8,128)(2,1)}, u32[]{:S(2)}) copy-start(bf16[128,1024]{0,1:T(8,128)(2,1)} %copy-done.4) | copy-start | bytes 786436
Sparse Core Ops, SparseCore 0:
  64.5 24.2 all-gather.4
  90.4 25.5 all-gather.6
  118.5 34.6 reduce-scatter.3
